TPU v7x, 32 devices: a whole 2x2x4 slice. The times are simulated.
32 devices in a mesh: groups: 2 (over y), section: 2 (over x), band: 4 (over z), chan: 2 (over core).
Axes of the slice: x: 2, y: 2, z: 4, core: 2. Of those that a mesh axis runs over, the one named last changes fastest.
Arguments:
- latent: bfloat16 [16, 128, 640], P(('groups', 'band'), None, ('section', 'chan')), parts along dimension 0, may hold values from -6 to 6
- control_hint: bfloat16 [16, 128, 640], P(('groups', 'band'), None, ('section', 'chan')), parts along dimension 0, may hold values from -6 to 6
- control_weight_one: bfloat16 [3, 3, 640, 640], P(None, None, ('section', 'chan')), may hold values from -0.078125 to 0.078125
- control_bias_one: bfloat16 [640], P(('section', 'chan')), may hold values from -3 to 3
- control_weight_two: bfloat16 [3, 3, 640, 640], P(None, None, ('section', 'chan')), may hold values from -0.078125 to 0.078125
- control_bias_two: bfloat16 [640], P(('section', 'chan')), may hold values from -3 to 3
- main_weight_one: bfloat16 [3, 3, 640, 640], P(None, None, ('section', 'chan')), may hold values from -0.078125 to 0.078125
- main_bias_one: bfloat16 [640], P(('section', 'chan')), may hold values from -3 to 3
- main_weight_two: bfloat16 [3, 3, 640, 640], P(None, None, ('section', 'chan')), may hold values from -0.078125 to 0.078125
- main_bias_two: bfloat16 [640], P(('section', 'chan')), may hold values from -3 to 3
- decoder_weight_one: bfloat16 [3, 3, 640, 1280], P(None, None, ('section', 'chan')), may hold values from -0.0546875 to 0.0546875
- decoder_bias_one: bfloat16 [640], P(('section', 'chan')), may hold values from -3 to 3
- decoder_weight_two: bfloat16 [3, 3, 640, 1280], P(None, None, ('section', 'chan')), may hold values from -0.0546875 to 0.0546875
- decoder_bias_two: bfloat16 [640], P(('section', 'chan')), may hold values from -3 to 3
Outputs:
- decoded: bfloat16 [16, 128, 640], P(('groups', 'band'), None, ('section', 'chan')), parts along dimension 0
There are 2 independent parts, one for each index of `groups`. A program takes and returns all parts, laid end to end along the dimension named above; an argument that names none is the same for every part. Nothing has to cross between parts.
All inputs are finite; a program needn't handle non-finite values.
Results may differ from a plain program's by a relative error of at most 0.015.
Values may be sent and summed in bfloat16 or wider, within the bound.
No kernel may reach another device: no remote copies, remote signals or barrier semaphores. Data moves between devices by JAX's collectives and lax.ppermute only.
A program may use at most 64 MiB of HBM per device.

v0:
```python
import jax
import jax.numpy as jnp
from jax import lax
from jax.sharding import PartitionSpec as P

C = 640


def padded_2(cells, sides, width):
    for axis, dim in sides:
        count = lax.axis_size(axis)
        ends = count - 1
        head = lax.slice_in_dim(cells, 0, width, axis=dim)
        tail = lax.slice_in_dim(cells, cells.shape[dim] - width, cells.shape[dim], axis=dim)
        cells = jnp.concatenate(
            [
                lax.ppermute(tail, axis, [(i, (i + 1) % count) for i in range(ends)]),
                cells,
                lax.ppermute(head, axis, [((i + 1) % count, i) for i in range(ends)]),
            ],
            axis=dim,
        )
    return cells


def activate(state):
    value = state.astype(jnp.float32)
    return (value * jax.nn.sigmoid(value)).astype(jnp.bfloat16)


def add_taps(running, portion, anchor, weights):
    height = portion.shape[0] - 2
    breadth = portion.shape[1]
    depth = portion.shape[2]
    outputs = weights.shape[2]
    kernel = lax.dynamic_slice_in_dim(weights, anchor, depth, 3)
    kernel = jnp.transpose(kernel, (3, 0, 1, 2)).reshape(depth, 9 * outputs)
    product = jnp.dot(
        portion.reshape((height + 2) * breadth, depth), kernel, preferred_element_type=jnp.float32
    )
    product = product.reshape(height + 2, breadth, 9 * outputs)
    padded = jnp.pad(product, ((0, 0), (1, 1), (0, 0)))
    for row_step in range(3):
        for col_step in range(3):
            tap_index = row_step * 3 + col_step
            running = (
                running
                + padded[
                    row_step : row_step + height,
                    col_step : col_step + breadth,
                    tap_index * outputs : (tap_index + 1) * outputs,
                ]
            )
    return running


def convolve(activated, weights, skip_bordered):
    height, breadth = (activated.shape[0], activated.shape[1])
    outputs = weights.shape[2]
    empty = jnp.zeros((height, breadth, outputs), jnp.float32)
    bordered = padded_2(activated, (("band", 0),), 1)
    running = add_taps(
        empty,
        lax.all_gather(bordered, ("section", "chan"), axis=2, tiled=True),
        jnp.int32(0),
        weights,
    )
    if skip_bordered is not None:
        running = add_taps(running, skip_bordered, C, weights)
    return running


def residual_layer(state, weights, offset, skip_bordered):
    activated = activate(state)
    result = convolve(activated, weights, skip_bordered)
    total = state.astype(jnp.float32) + result + offset.astype(jnp.float32)
    return total.astype(jnp.bfloat16)


def per_device(
    latent,
    control_hint,
    control_weight_one,
    control_bias_one,
    control_weight_two,
    control_bias_two,
    main_weight_one,
    main_bias_one,
    main_weight_two,
    main_bias_two,
    decoder_weight_one,
    decoder_bias_one,
    decoder_weight_two,
    decoder_bias_two,
):
    control_input = (latent.astype(jnp.float32) + control_hint.astype(jnp.float32)).astype(
        jnp.bfloat16
    )
    control_mid = residual_layer(control_input, control_weight_one, control_bias_one, None)
    control_out = residual_layer(control_mid, control_weight_two, control_bias_two, None)
    main_mid = residual_layer(latent, main_weight_one, main_bias_one, None)
    main_out = residual_layer(main_mid, main_weight_two, main_bias_two, None)
    control_act = activate(control_out)
    skip_whole = lax.all_gather(control_act, ("section", "chan"), axis=2, tiled=True)
    skip_bordered = padded_2(skip_whole, (("band", 0),), 1)
    decoder_mid = residual_layer(main_out, decoder_weight_one, decoder_bias_one, skip_bordered)
    decoded = residual_layer(decoder_mid, decoder_weight_two, decoder_bias_two, skip_bordered)
    return decoded


def solution(mesh):
    placed = (
        P(("groups", "band"), None, ("section", "chan")),
        P(("groups", "band"), None, ("section", "chan")),
        P(None, None, ("section", "chan"), None),
        P(("section", "chan")),
        P(None, None, ("section", "chan"), None),
        P(("section", "chan")),
        P(None, None, ("section", "chan"), None),
        P(("section", "chan")),
        P(None, None, ("section", "chan"), None),
        P(("section", "chan")),
        P(None, None, ("section", "chan"), None),
        P(("section", "chan")),
        P(None, None, ("section", "chan"), None),
        P(("section", "chan")),
    )
    return jax.shard_map(
        per_device,
        mesh=mesh,
        in_specs=placed,
        out_specs=P(("groups", "band"), None, ("section", "chan")),
        check_vma=False,
    )
```

profile of v0, /device:TPU:0, one launch (start us, length us, event | category | flops | bytes accessed | tf_op | source)
XLA Modules:
  0.0 116.4 jit_solution(5973519125874029904)
XLA Ops:
  0.0 1.2 fusion.103
  1.2 5.0 %collective-permute-start = (bf16[1,128,160]{1,2,0:T(8,128)(2,1)S(1)}, bf16[1,128,160]{1,2,0:T(8,128)(2,1)S(1)}, u32[]{:S(2)}, u32[]{:S(2)}) collective-permute-start(bf16[1,128,160]{1,2,0:T(8,128)(2,1)S(1)} %get-tuple-element.27), channel_id=1, source_target_pairs={{0,2},{2,4},{4,6},{1,3},{3,5},{5,7},{8,10},{10,12},{12,14},{9,11},... | collective-permute-start | bytes 122888 | tf_op jit(solution)/shard_map/ppermute | solution.py:17
  6.1 1.3 %collective-permute-start.1 = (bf16[1,128,160]{1,2,0:T(8,128)(2,1)S(1)}, bf16[1,128,160]{1,2,0:T(8,128)(2,1)S(1)}, u32[]{:S(2)}, u32[]{:S(2)}) collective-permute-start(bf16[1,128,160]{1,2,0:T(8,128)(2,1)S(1)} %get-tuple-element.28), channel_id=1, source_target_pairs={{2,0},{4,2},{6,4},{3,1},{5,3},{7,5},{10,8},{12,10},{14,12},{11,9},... | collective-permute-start | bytes 122888 | tf_op jit(solution)/shard_map/ppermute | solution.py:19
  7.5 4.5 %collective-permute-start.6 = (bf16[1,128,160]{1,2,0:T(8,128)(2,1)S(1)}, bf16[1,128,160]{1,2,0:T(8,128)(2,1)S(1)}, u32[]{:S(2)}, u32[]{:S(2)}) collective-permute-start(bf16[1,128,160]{1,2,0:T(8,128)(2,1)S(1)} %get-tuple-element.33), channel_id=1, source_target_pairs={{0,2},{2,4},{4,6},{1,3},{3,5},{5,7},{8,10},{10,12},{12,14},{9,11},... | collective-permute-start | bytes 122888 | tf_op jit(solution)/shard_map/ppermute | solution.py:17
  12.0 0.0 copy-start.1
  12.0 1.6 %collective-permute-start.7 = (bf16[1,128,160]{1,2,0:T(8,128)(2,1)S(1)}, bf16[1,128,160]{1,2,0:T(8,128)(2,1)S(1)}, u32[]{:S(2)}, u32[]{:S(2)}) collective-permute-start(bf16[1,128,160]{1,2,0:T(8,128)(2,1)S(1)} %get-tuple-element.34), channel_id=1, source_target_pairs={{2,0},{4,2},{6,4},{3,1},{5,3},{7,5},{10,8},{12,10},{14,12},{11,9},... | collective-permute-start | bytes 122888 | tf_op jit(solution)/shard_map/ppermute | solution.py:19
  13.6 2.4 %fusion.112 = (bf16[3,3,160,640]{3,2,1,0:T(8,128)(2,1)S(1)}, bf16[3,3,160,640]{3,2,1,0:T(8,128)(2,1)S(1)}) fusion(bf16[3,3,160,1280]{3,2,1,0:T(8,128)(2,1)} %param.24), kind=kLoop, calls=%fused_computation.186 | loop fusion | bytes 7372800 | tf_op jit(solution)/shard_map/dynamic_slice | solution.py:36
  16.0 0.0 copy-start.7
  16.1 0.3 fusion.111
  16.4 0.3 copy-done.7
  16.7 0.0 copy-done.8
  16.7 0.0 copy-done.9
  16.7 0.0 copy-done.10
  16.7 0.0 copy-done.11
  16.7 0.0 copy-done.12
  16.7 1.4 %collective-permute-done.7 = bf16[1,128,160]{1,2,0:T(8,128)(2,1)S(1)} collective-permute-done((bf16[1,128,160]{1,2,0:T(8,128)(2,1)S(1)}, bf16[1,128,160]{1,2,0:T(8,128)(2,1)S(1)}, u32[]{:S(2)}, u32[]{:S(2)}) %collective-permute-start.7) | collective-permute-done | bytes 40992 | tf_op jit(solution)/shard_map/ppermute | solution.py:19
  18.2 7.9 %all_gather.24 = bf16[4,128,640]{1,2,0:T(8,128)(2,1)S(1)} all-gather(bf16[4,128,160]{1,2,0:T(8,128)(2,1)S(1)} %pad_maximum_fusion.3), channel_id=1, replica_groups=mesh['groups'=2,'section'=2,'band'=4,'chan'=2] {'section','chan'}, dimensions={2}, use_global_device_ids=true | all-gather | bytes 819200 | tf_op jit(solution)/shard_map/all_gather | solution.py:64
  26.1 8.0 %all_gather.21 = bf16[4,128,640]{1,2,0:T(8,128)(2,1)S(1)} all-gather(bf16[4,128,160]{1,2,0:T(8,128)(2,1)S(1)} %pad_maximum_fusion), channel_id=1, replica_groups=mesh['groups'=2,'section'=2,'band'=4,'chan'=2] {'section','chan'}, dimensions={2}, use_global_device_ids=true | all-gather | bytes 819200 | tf_op jit(solution)/shard_map/all_gather | solution.py:64
  34.1 1.3 %fusion.120 = f32[4,128,1440]{1,2,0:T(8,128)S(1)} fusion(bf16[640,1440,1]{0,1,2:T(8,128)(2,1)S(1)} %bitcast.56, bf16[4,128,640]{1,2,0:T(8,128)(2,1)S(1)} %all_gather.21), kind=kOutput, calls=%fused_computation.194 | convolution fusion | flops 943718400 | bytes 5447680 | tf_op jit(solution)/shard_map/dot_general | solution.py:38
  35.5 0.2 copy-done.4
  35.6 1.3 %fusion.123 = f32[4,128,1440]{1,2,0:T(8,128)S(1)} fusion(bf16[640,1440,1]{0,1,2:T(8,128)(2,1)S(1)} %bitcast.61, bf16[4,128,640]{1,2,0:T(8,128)(2,1)S(1)} %all_gather.24), kind=kOutput, calls=%fused_computation.197 | convolution fusion | flops 943718400 | bytes 5447680 | tf_op jit(solution)/shard_map/dot_general | solution.py:38
  37.0 0.6 fusion.73
  37.6 3.5 %collective-permute-start.8 = (bf16[1,128,160]{1,2,0:T(8,128)(2,1)S(1)}, bf16[1,128,160]{1,2,0:T(8,128)(2,1)S(1)}, u32[]{:S(2)}, u32[]{:S(2)}) collective-permute-start(bf16[1,128,160]{1,2,0:T(8,128)(2,1)S(1)} %get-tuple-element.31), channel_id=1, source_target_pairs={{0,2},{2,4},{4,6},{1,3},{3,5},{5,7},{8,10},{10,12},{12,14},{9,11},... | collective-permute-start | bytes 122888 | tf_op jit(solution)/shard_map/ppermute | solution.py:17
  41.1 1.3 %collective-permute-start.9 = (bf16[1,128,160]{1,2,0:T(8,128)(2,1)S(1)}, bf16[1,128,160]{1,2,0:T(8,128)(2,1)S(1)}, u32[]{:S(2)}, u32[]{:S(2)}) collective-permute-start(bf16[1,128,160]{1,2,0:T(8,128)(2,1)S(1)} %get-tuple-element.32), channel_id=1, source_target_pairs={{2,0},{4,2},{6,4},{3,1},{5,3},{7,5},{10,8},{12,10},{14,12},{11,9},... | collective-permute-start | bytes 122888 | tf_op jit(solution)/shard_map/ppermute | solution.py:19
  42.5 4.5 %collective-permute-start.2 = (bf16[1,128,160]{1,2,0:T(8,128)(2,1)S(1)}, bf16[1,128,160]{1,2,0:T(8,128)(2,1)S(1)}, u32[]{:S(2)}, u32[]{:S(2)}) collective-permute-start(bf16[1,128,160]{1,2,0:T(8,128)(2,1)S(1)} %get-tuple-element.23), channel_id=1, source_target_pairs={{0,2},{2,4},{4,6},{1,3},{3,5},{5,7},{8,10},{10,12},{12,14},{9,11},... | collective-permute-start | bytes 122888 | tf_op jit(solution)/shard_map/ppermute | solution.py:17
  47.0 1.3 %collective-permute-start.3 = (bf16[1,128,160]{1,2,0:T(8,128)(2,1)S(1)}, bf16[1,128,160]{1,2,0:T(8,128)(2,1)S(1)}, u32[]{:S(2)}, u32[]{:S(2)}) collective-permute-start(bf16[1,128,160]{1,2,0:T(8,128)(2,1)S(1)} %get-tuple-element.24), channel_id=1, source_target_pairs={{2,0},{4,2},{6,4},{3,1},{5,3},{7,5},{10,8},{12,10},{14,12},{11,9},... | collective-permute-start | bytes 122888 | tf_op jit(solution)/shard_map/ppermute | solution.py:19
  48.4 7.2 %all_gather.25 = bf16[4,128,640]{1,2,0:T(8,128)(2,1)S(1)} all-gather(bf16[4,128,160]{1,2,0:T(8,128)(2,1)S(1)} %pad_maximum_fusion.4), channel_id=1, replica_groups=mesh['groups'=2,'section'=2,'band'=4,'chan'=2] {'section','chan'}, dimensions={2}, use_global_device_ids=true | all-gather | bytes 819200 | tf_op jit(solution)/shard_map/all_gather | solution.py:64
  55.6 8.0 %all_gather.22 = bf16[4,128,640]{1,2,0:T(8,128)(2,1)S(1)} all-gather(bf16[4,128,160]{1,2,0:T(8,128)(2,1)S(1)} %pad_maximum_fusion.1), channel_id=1, replica_groups=mesh['groups'=2,'section'=2,'band'=4,'chan'=2] {'section','chan'}, dimensions={2}, use_global_device_ids=true | all-gather | bytes 819200 | tf_op jit(solution)/shard_map/all_gather | solution.py:64
  63.6 1.3 %fusion.121 = f32[4,128,1440]{1,2,0:T(8,128)S(1)} fusion(bf16[640,1440,1]{0,1,2:T(8,128)(2,1)S(1)} %bitcast.62, bf16[4,128,640]{1,2,0:T(8,128)(2,1)S(1)} %all_gather.22), kind=kOutput, calls=%fused_computation.195 | convolution fusion | flops 943718400 | bytes 5447680 | tf_op jit(solution)/shard_map/dot_general | solution.py:38
  64.9 0.4 fusion.79
  65.3 4.5 %collective-permute-start.4 = (bf16[1,128,160]{1,2,0:T(8,128)(2,1)S(1)}, bf16[1,128,160]{1,2,0:T(8,128)(2,1)S(1)}, u32[]{:S(2)}, u32[]{:S(2)}) collective-permute-start(bf16[1,128,160]{1,2,0:T(8,128)(2,1)S(1)} %get-tuple-element.21), channel_id=1, source_target_pairs={{0,2},{2,4},{4,6},{1,3},{3,5},{5,7},{8,10},{10,12},{12,14},{9,11},... | collective-permute-start | bytes 122888 | tf_op jit(solution)/shard_map/ppermute | solution.py:17
  69.7 1.3 %collective-permute-start.5 = (bf16[1,128,160]{1,2,0:T(8,128)(2,1)S(1)}, bf16[1,128,160]{1,2,0:T(8,128)(2,1)S(1)}, u32[]{:S(2)}, u32[]{:S(2)}) collective-permute-start(bf16[1,128,160]{1,2,0:T(8,128)(2,1)S(1)} %get-tuple-element.22), channel_id=1, source_target_pairs={{2,0},{4,2},{6,4},{3,1},{5,3},{7,5},{10,8},{12,10},{14,12},{11,9},... | collective-permute-start | bytes 122888 | tf_op jit(solution)/shard_map/ppermute | solution.py:19
  71.0 1.3 %fusion.124 = f32[4,128,1440]{1,2,0:T(8,128)S(1)} fusion(bf16[640,1440,1]{0,1,2:T(8,128)(2,1)S(1)} %bitcast.63, bf16[4,128,640]{1,2,0:T(8,128)(2,1)S(1)} %all_gather.25), kind=kOutput, calls=%fused_computation.198 | convolution fusion | flops 943718400 | bytes 5447680 | tf_op jit(solution)/shard_map/dot_general | solution.py:38
  72.4 0.4 fusion.69
  72.7 6.1 %all_gather.26 = bf16[2,128,640]{1,2,0:T(8,128)(2,1)S(1)} all-gather(bf16[2,128,160]{1,2,0:T(8,128)(2,1)S(1)} %fusion.69), channel_id=1, replica_groups=mesh['groups'=2,'section'=2,'band'=4,'chan'=2] {'section','chan'}, dimensions={2}, use_global_device_ids=true | all-gather | bytes 409600 | tf_op jit(solution)/shard_map/all_gather | solution.py:104
  78.9 1.3 %collective-permute-start.11 = (bf16[1,128,640]{1,2,0:T(8,128)(2,1)S(1)}, bf16[1,128,640]{1,2,0:T(8,128)(2,1)S(1)}, u32[]{:S(2)}, u32[]{:S(2)}) collective-permute-start(bf16[1,128,640]{1,2,0:T(8,128)(2,1)S(1)} %get-tuple-element.17), channel_id=1, source_target_pairs={{2,0},{4,2},{6,4},{3,1},{5,3},{7,5},{10,8},{12,10},{14,12},{11,9},... | collective-permute-start | bytes 491528 | tf_op jit(solution)/shard_map/ppermute | solution.py:19
  80.2 5.2 %collective-permute-start.10 = (bf16[1,128,640]{1,2,0:T(8,128)(2,1)S(1)}, bf16[1,128,640]{1,2,0:T(8,128)(2,1)S(1)}, u32[]{:S(2)}, u32[]{:S(2)}) collective-permute-start(bf16[1,128,640]{1,2,0:T(8,128)(2,1)S(1)} %get-tuple-element.18), channel_id=1, source_target_pairs={{0,2},{2,4},{4,6},{1,3},{3,5},{5,7},{8,10},{10,12},{12,14},{9,11},... | collective-permute-start | bytes 491528 | tf_op jit(solution)/shard_map/ppermute | solution.py:17
  85.4 7.7 %all_gather.23 = bf16[4,128,640]{1,2,0:T(8,128)(2,1)S(1)} all-gather(bf16[4,128,160]{1,2,0:T(8,128)(2,1)S(1)} %pad_maximum_fusion.2), channel_id=1, replica_groups=mesh['groups'=2,'section'=2,'band'=4,'chan'=2] {'section','chan'}, dimensions={2}, use_global_device_ids=true | all-gather | bytes 819200 | tf_op jit(solution)/shard_map/all_gather | solution.py:64
  93.1 1.3 %fusion.122 = f32[4,128,1440]{1,2,0:T(8,128)S(1)} fusion(bf16[640,1440,1]{0,1,2:T(8,128)(2,1)S(1)} %bitcast.60, bf16[4,128,640]{1,2,0:T(8,128)(2,1)S(1)} %all_gather.23), kind=kOutput, calls=%fused_computation.196 | convolution fusion | flops 943718400 | bytes 5447680 | tf_op jit(solution)/shard_map/dot_general | solution.py:38
  94.6 1.3 %fusion.125 = f32[4,128,1440]{1,2,0:T(8,128)S(1)} fusion(bf16[640,1440,1]{0,1,2:T(8,128)(2,1)S(1)} %bitcast.59, bf16[4,128,640]{1,2,0:T(8,128)(2,1)S(1)} %constant_dynamic-update-slice_fusion), kind=kOutput, calls=%fused_computation.199 | convolution fusion | flops 943718400 | bytes 5447680 | tf_op jit(solution)/shard_map/dot_general | solution.py:38
  95.9 0.6 fusion.97
  96.6 3.9 %collective-permute-start.12 = (bf16[1,128,160]{1,2,0:T(8,128)(2,1)S(1)}, bf16[1,128,160]{1,2,0:T(8,128)(2,1)S(1)}, u32[]{:S(2)}, u32[]{:S(2)}) collective-permute-start(bf16[1,128,160]{1,2,0:T(8,128)(2,1)S(1)} %get-tuple-element.19), channel_id=1, source_target_pairs={{0,2},{2,4},{4,6},{1,3},{3,5},{5,7},{8,10},{10,12},{12,14},{9,11},... | collective-permute-start | bytes 122888 | tf_op jit(solution)/shard_map/ppermute | solution.py:17
  100.5 1.5 %collective-permute-start.13 = (bf16[1,128,160]{1,2,0:T(8,128)(2,1)S(1)}, bf16[1,128,160]{1,2,0:T(8,128)(2,1)S(1)}, u32[]{:S(2)}, u32[]{:S(2)}) collective-permute-start(bf16[1,128,160]{1,2,0:T(8,128)(2,1)S(1)} %get-tuple-element.20), channel_id=1, source_target_pairs={{2,0},{4,2},{6,4},{3,1},{5,3},{7,5},{10,8},{12,10},{14,12},{11,9},... | collective-permute-start | bytes 122888 | tf_op jit(solution)/shard_map/ppermute | solution.py:19
  102.0 1.3 %fusion.127 = f32[4,128,1440]{1,2,0:T(8,128)S(1)} fusion(bf16[640,1440,1]{0,1,2:T(8,128)(2,1)S(1)} %bitcast.58, bf16[4,128,640]{1,2,0:T(8,128)(2,1)S(1)} %constant_dynamic-update-slice_fusion), kind=kOutput, calls=%fused_computation.201 | convolution fusion | flops 943718400 | bytes 5447680 | tf_op jit(solution)/shard_map/dot_general | solution.py:38
  103.3 3.1 %collective-permute-done.13 = bf16[1,128,160]{1,2,0:T(8,128)(2,1)S(1)} collective-permute-done((bf16[1,128,160]{1,2,0:T(8,128)(2,1)S(1)}, bf16[1,128,160]{1,2,0:T(8,128)(2,1)S(1)}, u32[]{:S(2)}, u32[]{:S(2)}) %collective-permute-start.13) | collective-permute-done | bytes 40992 | tf_op jit(solution)/shard_map/ppermute | solution.py:19
  106.4 7.4 %all_gather.27 = bf16[4,128,640]{1,2,0:T(8,128)(2,1)S(1)} all-gather(bf16[4,128,160]{1,2,0:T(8,128)(2,1)S(1)} %pad_maximum_fusion.5), channel_id=1, replica_groups=mesh['groups'=2,'section'=2,'band'=4,'chan'=2] {'section','chan'}, dimensions={2}, use_global_device_ids=true | all-gather | bytes 819200 | tf_op jit(solution)/shard_map/all_gather | solution.py:64
  113.8 1.3 %fusion.126 = f32[4,128,1440]{1,2,0:T(8,128)S(1)} fusion(bf16[640,1440,1]{0,1,2:T(8,128)(2,1)S(1)} %bitcast.57, bf16[4,128,640]{1,2,0:T(8,128)(2,1)S(1)} %all_gather.27), kind=kOutput, calls=%fused_computation.200 | convolution fusion | flops 943718400 | bytes 5447680 | tf_op jit(solution)/shard_map/dot_general | solution.py:38
  115.1 1.2 %fusion.99 = bf16[2,128,160]{1,2,0:T(8,128)(2,1)} fusion(bf16[2,128,160]{1,2,0:T(8,128)(2,1)S(1)} %get-tuple-element.6, f32[4,128,1440]{1,2,0:T(8,128)S(1)} %fusion.127, f32[4,128,1440]{1,2,0:T(8,128)S(1)} %fusion.126, f32[160]{0:T(256)S(1)} %convert_element_type.126), kind=kLoop, calls=%fused_computation.168 | loop fusion | flops 860160 | bytes 7046144 | tf_op jit(solution)/shard_map/convert_element_type | solution.py:77
  (51 shorter events, 0.4 us)
Async XLA Ops:
  0.0 34.1 %copy-start = (bf16[3,3,160,640]{3,2,1,0:T(8,128)(2,1)S(1)}, bf16[3,3,160,640]{3,2,1,0:T(8,128)(2,1)}, u32[]{:S(2)}) copy-start(bf16[3,3,160,640]{3,2,1,0:T(8,128)(2,1)} %param.20) | copy-start | bytes 5529604
  1.2 24.9 %collective-permute-start = (bf16[1,128,160]{1,2,0:T(8,128)(2,1)S(1)}, bf16[1,128,160]{1,2,0:T(8,128)(2,1)S(1)}, u32[]{:S(2)}, u32[]{:S(2)}) collective-permute-start(bf16[1,128,160]{1,2,0:T(8,128)(2,1)S(1)} %get-tuple-element.27), channel_id=1, source_target_pairs={{0,2},{2,4},{4,6},{1,3},{3,5},{5,7},{8,10},{10,12},{12,14},{9,11},... | collective-permute-start | bytes 122888 | tf_op jit(solution)/shard_map/ppermute | solution.py:17
  6.1 20.0 %collective-permute-start.1 = (bf16[1,128,160]{1,2,0:T(8,128)(2,1)S(1)}, bf16[1,128,160]{1,2,0:T(8,128)(2,1)S(1)}, u32[]{:S(2)}, u32[]{:S(2)}) collective-permute-start(bf16[1,128,160]{1,2,0:T(8,128)(2,1)S(1)} %get-tuple-element.28), channel_id=1, source_target_pairs={{2,0},{4,2},{6,4},{3,1},{5,3},{7,5},{10,8},{12,10},{14,12},{11,9},... | collective-permute-start | bytes 122888 | tf_op jit(solution)/shard_map/ppermute | solution.py:19
  7.5 9.3 %collective-permute-start.6 = (bf16[1,128,160]{1,2,0:T(8,128)(2,1)S(1)}, bf16[1,128,160]{1,2,0:T(8,128)(2,1)S(1)}, u32[]{:S(2)}, u32[]{:S(2)}) collective-permute-start(bf16[1,128,160]{1,2,0:T(8,128)(2,1)S(1)} %get-tuple-element.33), channel_id=1, source_target_pairs={{0,2},{2,4},{4,6},{1,3},{3,5},{5,7},{8,10},{10,12},{12,14},{9,11},... | collective-permute-start | bytes 122888 | tf_op jit(solution)/shard_map/ppermute | solution.py:17
  12.0 4.0 %copy-start.1 = (bf16[3,3,160,1280]{3,2,1,0:T(8,128)(2,1)S(1)}, bf16[3,3,160,1280]{3,2,1,0:T(8,128)(2,1)}, u32[]{:S(2)}) copy-start(bf16[3,3,160,1280]{3,2,1,0:T(8,128)(2,1)} %param.26) | copy-start | bytes 11059204
  12.0 6.2 %collective-permute-start.7 = (bf16[1,128,160]{1,2,0:T(8,128)(2,1)S(1)}, bf16[1,128,160]{1,2,0:T(8,128)(2,1)S(1)}, u32[]{:S(2)}, u32[]{:S(2)}) collective-permute-start(bf16[1,128,160]{1,2,0:T(8,128)(2,1)S(1)} %get-tuple-element.34), channel_id=1, source_target_pairs={{2,0},{4,2},{6,4},{3,1},{5,3},{7,5},{10,8},{12,10},{14,12},{11,9},... | collective-permute-start | bytes 122888 | tf_op jit(solution)/shard_map/ppermute | solution.py:19
  16.0 0.7 copy-start.7
  16.0 0.7 copy-start.8
  16.0 0.7 copy-start.9
  16.0 0.7 copy-start.10
  16.0 0.7 copy-start.11
  16.0 0.7 copy-start.12
  34.1 1.5 %copy-start.4 = (bf16[3,3,160,640]{3,2,1,0:T(8,128)(2,1)S(1)}, bf16[3,3,160,640]{3,2,1,0:T(8,128)(2,1)}, u32[]{:S(2)}) copy-start(bf16[3,3,160,640]{3,2,1,0:T(8,128)(2,1)} %param.16) | copy-start | bytes 5529604
  35.4 1.5 %copy-start.2 = (bf16[2,128,160]{1,2,0:T(8,128)(2,1)S(1)}, bf16[2,128,160]{1,2,0:T(8,128)(2,1)}, u32[]{:S(2)}) copy-start(bf16[2,128,160]{1,2,0:T(8,128)(2,1)} %param.14) | copy-start | bytes 245764
  35.5 1.5 %copy-start.3 = (bf16[2,128,160]{1,2,0:T(8,128)(2,1)S(1)}, bf16[2,128,160]{1,2,0:T(8,128)(2,1)}, u32[]{:S(2)}) copy-start(bf16[2,128,160]{1,2,0:T(8,128)(2,1)} %param.15) | copy-start | bytes 245764
  37.0 26.6 %copy-start.5 = (bf16[3,3,160,640]{3,2,1,0:T(8,128)(2,1)S(1)}, bf16[3,3,160,640]{3,2,1,0:T(8,128)(2,1)}, u32[]{:S(2)}) copy-start(bf16[3,3,160,640]{3,2,1,0:T(8,128)(2,1)} %param.22) | copy-start | bytes 5529604
  37.6 10.7 %collective-permute-start.8 = (bf16[1,128,160]{1,2,0:T(8,128)(2,1)S(1)}, bf16[1,128,160]{1,2,0:T(8,128)(2,1)S(1)}, u32[]{:S(2)}, u32[]{:S(2)}) collective-permute-start(bf16[1,128,160]{1,2,0:T(8,128)(2,1)S(1)} %get-tuple-element.31), channel_id=1, source_target_pairs={{0,2},{2,4},{4,6},{1,3},{3,5},{5,7},{8,10},{10,12},{12,14},{9,11},... | collective-permute-start | bytes 122888 | tf_op jit(solution)/shard_map/ppermute | solution.py:17
  41.1 7.2 %collective-permute-start.9 = (bf16[1,128,160]{1,2,0:T(8,128)(2,1)S(1)}, bf16[1,128,160]{1,2,0:T(8,128)(2,1)S(1)}, u32[]{:S(2)}, u32[]{:S(2)}) collective-permute-start(bf16[1,128,160]{1,2,0:T(8,128)(2,1)S(1)} %get-tuple-element.32), channel_id=1, source_target_pairs={{2,0},{4,2},{6,4},{3,1},{5,3},{7,5},{10,8},{12,10},{14,12},{11,9},... | collective-permute-start | bytes 122888 | tf_op jit(solution)/shard_map/ppermute | solution.py:19
  42.5 13.1 %collective-permute-start.2 = (bf16[1,128,160]{1,2,0:T(8,128)(2,1)S(1)}, bf16[1,128,160]{1,2,0:T(8,128)(2,1)S(1)}, u32[]{:S(2)}, u32[]{:S(2)}) collective-permute-start(bf16[1,128,160]{1,2,0:T(8,128)(2,1)S(1)} %get-tuple-element.23), channel_id=1, source_target_pairs={{0,2},{2,4},{4,6},{1,3},{3,5},{5,7},{8,10},{10,12},{12,14},{9,11},... | collective-permute-start | bytes 122888 | tf_op jit(solution)/shard_map/ppermute | solution.py:17
  47.0 8.5 %collective-permute-start.3 = (bf16[1,128,160]{1,2,0:T(8,128)(2,1)S(1)}, bf16[1,128,160]{1,2,0:T(8,128)(2,1)S(1)}, u32[]{:S(2)}, u32[]{:S(2)}) collective-permute-start(bf16[1,128,160]{1,2,0:T(8,128)(2,1)S(1)} %get-tuple-element.24), channel_id=1, source_target_pairs={{2,0},{4,2},{6,4},{3,1},{5,3},{7,5},{10,8},{12,10},{14,12},{11,9},... | collective-permute-start | bytes 122888 | tf_op jit(solution)/shard_map/ppermute | solution.py:19
  64.9 6.2 %copy-start.6 = (bf16[3,3,160,640]{3,2,1,0:T(8,128)(2,1)S(1)}, bf16[3,3,160,640]{3,2,1,0:T(8,128)(2,1)}, u32[]{:S(2)}) copy-start(bf16[3,3,160,640]{3,2,1,0:T(8,128)(2,1)} %param.18) | copy-start | bytes 5529604
  65.3 20.1 %collective-permute-start.4 = (bf16[1,128,160]{1,2,0:T(8,128)(2,1)S(1)}, bf16[1,128,160]{1,2,0:T(8,128)(2,1)S(1)}, u32[]{:S(2)}, u32[]{:S(2)}) collective-permute-start(bf16[1,128,160]{1,2,0:T(8,128)(2,1)S(1)} %get-tuple-element.21), channel_id=1, source_target_pairs={{0,2},{2,4},{4,6},{1,3},{3,5},{5,7},{8,10},{10,12},{12,14},{9,11},... | collective-permute-start | bytes 122888 | tf_op jit(solution)/shard_map/ppermute | solution.py:17
  69.7 15.6 %collective-permute-start.5 = (bf16[1,128,160]{1,2,0:T(8,128)(2,1)S(1)}, bf16[1,128,160]{1,2,0:T(8,128)(2,1)S(1)}, u32[]{:S(2)}, u32[]{:S(2)}) collective-permute-start(bf16[1,128,160]{1,2,0:T(8,128)(2,1)S(1)} %get-tuple-element.22), channel_id=1, source_target_pairs={{2,0},{4,2},{6,4},{3,1},{5,3},{7,5},{10,8},{12,10},{14,12},{11,9},... | collective-permute-start | bytes 122888 | tf_op jit(solution)/shard_map/ppermute | solution.py:19
  78.9 15.7 %collective-permute-start.11 = (bf16[1,128,640]{1,2,0:T(8,128)(2,1)S(1)}, bf16[1,128,640]{1,2,0:T(8,128)(2,1)S(1)}, u32[]{:S(2)}, u32[]{:S(2)}) collective-permute-start(bf16[1,128,640]{1,2,0:T(8,128)(2,1)S(1)} %get-tuple-element.17), channel_id=1, source_target_pairs={{2,0},{4,2},{6,4},{3,1},{5,3},{7,5},{10,8},{12,10},{14,12},{11,9},... | collective-permute-start | bytes 491528 | tf_op jit(solution)/shard_map/ppermute | solution.py:19
  80.2 14.3 %collective-permute-start.10 = (bf16[1,128,640]{1,2,0:T(8,128)(2,1)S(1)}, bf16[1,128,640]{1,2,0:T(8,128)(2,1)S(1)}, u32[]{:S(2)}, u32[]{:S(2)}) collective-permute-start(bf16[1,128,640]{1,2,0:T(8,128)(2,1)S(1)} %get-tuple-element.18), channel_id=1, source_target_pairs={{0,2},{2,4},{4,6},{1,3},{3,5},{5,7},{8,10},{10,12},{12,14},{9,11},... | collective-permute-start | bytes 491528 | tf_op jit(solution)/shard_map/ppermute | solution.py:17
  96.6 6.7 %collective-permute-start.12 = (bf16[1,128,160]{1,2,0:T(8,128)(2,1)S(1)}, bf16[1,128,160]{1,2,0:T(8,128)(2,1)S(1)}, u32[]{:S(2)}, u32[]{:S(2)}) collective-permute-start(bf16[1,128,160]{1,2,0:T(8,128)(2,1)S(1)} %get-tuple-element.19), channel_id=1, source_target_pairs={{0,2},{2,4},{4,6},{1,3},{3,5},{5,7},{8,10},{10,12},{12,14},{9,11},... | collective-permute-start | bytes 122888 | tf_op jit(solution)/shard_map/ppermute | solution.py:17
  100.5 5.9 %collective-permute-start.13 = (bf16[1,128,160]{1,2,0:T(8,128)(2,1)S(1)}, bf16[1,128,160]{1,2,0:T(8,128)(2,1)S(1)}, u32[]{:S(2)}, u32[]{:S(2)}) collective-permute-start(bf16[1,128,160]{1,2,0:T(8,128)(2,1)S(1)} %get-tuple-element.20), channel_id=1, source_target_pairs={{2,0},{4,2},{6,4},{3,1},{5,3},{7,5},{10,8},{12,10},{14,12},{11,9},... | collective-permute-start | bytes 122888 | tf_op jit(solution)/shard_map/ppermute | solution.py:19
where the time goes:
time: 117 us; the launch traced here: 116 us
  blocking collectives  52.3 us (45%)
  starting transfers between devices  40.6 us (35%)
  matrix products  10.5 us (9%)
  waiting for transfers between devices  4.56 us (4%)
  other arithmetic  4.51 us (4%)
  local copies, waits for them, and re-layouts  3.39 us (3%)
    all_gather x6, blocking collectives, convolve(): lax.all_gather(bordered, ('section', 'chan'), axis=2, tiled=True)  46.2 us
    ppermute x7, starting transfers between devices, padded_2(): lax.ppermute(tail, axis, [(i, (i + 1) % count) for i in range(ends)])  31.1 us
    dot_general x8, matrix products, add_taps(): jnp.dot(portion.reshape((height + 2) * breadth, depth), kernel, preferred...  10.5 us
    ppermute x7, starting transfers between devices, padded_2(): lax.ppermute(head, axis, [((i + 1) % count, i) for i in range(ends)])  9.49 us
    all_gather x1, blocking collectives, per_device(): lax.all_gather(control_act, ('section', 'chan'), axis=2, tiled=True)  6.1 us
    ppermute x7, waiting for transfers between devices, padded_2(): lax.ppermute(head, axis, [((i + 1) % count, i) for i in range(ends)])  4.54 us
    convert_element_type x5, other arithmetic, activate(): return (value * jax.nn.sigmoid(value)).astype(jnp.bfloat16)  3.12 us
    dynamic_slice x2, local copies, waits for them, and re-layouts, add_taps(): kernel = lax.dynamic_slice_in_dim(weights, anchor, depth, 3)  2.7 us
  transfers between devices with their start and end apart: 14, of which 2 were waited for; matrix products, arithmetic and copies ran while one was open for 6% of the time, Pallas kernels for 0%

commit v1 on v0

--- a/solution.py
+++ b/solution.py
@@ -4,6 +4,11 @@
 from jax.sharding import PartitionSpec as P
 
 C = 640
+
+
+def all_parts(x, axis, d):
+    blocks = lax.all_gather(x, axis)
+    return jnp.concatenate(blocks, axis=d)
 
 
 def padded_2(cells, sides, width):
@@ -59,12 +64,7 @@
     outputs = weights.shape[2]
     empty = jnp.zeros((height, breadth, outputs), jnp.float32)
     bordered = padded_2(activated, (("band", 0),), 1)
-    running = add_taps(
-        empty,
-        lax.all_gather(bordered, ("section", "chan"), axis=2, tiled=True),
-        jnp.int32(0),
-        weights,
-    )
+    running = add_taps(empty, all_parts(bordered, ("section", "chan"), 2), jnp.int32(0), weights)
     if skip_bordered is not None:
         running = add_taps(running, skip_bordered, C, weights)
     return running

time: 117 us -> 118 us (level)
  no operation moved by 1% of the time
where the time goes in v1:
time: 118 us; the launch traced here: 117 us
  blocking collectives  52.3 us (44%)
  starting transfers between devices  40.7 us (34%)
  matrix products  10.5 us (9%)
  waiting for transfers between devices  4.74 us (4%)
  other arithmetic  4.51 us (4%)
  local copies, waits for them, and re-layouts  3.64 us (3%)
    all_gather x6, blocking collectives, all_parts(): blocks = lax.all_gather(x, axis)  46.2 us
    ppermute x7, starting transfers between devices, padded_2(): lax.ppermute(tail, axis, [(i, (i + 1) % count) for i in range(ends)])  31.2 us
    dot_general x8, matrix products, add_taps(): jnp.dot(portion.reshape((height + 2) * breadth, depth), kernel, preferred...  10.5 us
    ppermute x7, starting transfers between devices, padded_2(): lax.ppermute(head, axis, [((i + 1) % count, i) for i in range(ends)])  9.49 us
    all_gather x1, blocking collectives, per_device(): lax.all_gather(control_act, ('section', 'chan'), axis=2, tiled=True)  6.1 us
    ppermute x7, waiting for transfers between devices, padded_2(): lax.ppermute(head, axis, [((i + 1) % count, i) for i in range(ends)])  4.72 us
    convert_element_type x5, other arithmetic, activate(): return (value * jax.nn.sigmoid(value)).astype(jnp.bfloat16)  3.12 us
    dynamic_slice x2, local copies, waits for them, and re-layouts, add_taps(): kernel = lax.dynamic_slice_in_dim(weights, anchor, depth, 3)  2.7 us
  transfers between devices with their start and end apart: 14, of which 2 were waited for; matrix products, arithmetic and copies ran while one was open for 6% of the time, Pallas kernels for 0%

profile of v1, /device:TPU:0, one launch (start us, length us, event | category | flops | bytes accessed | tf_op | source)
XLA Modules:
  0.0 117.0 jit_solution(10713641388621007541)
XLA Ops:
  0.0 1.2 fusion.103
  1.2 5.0 %collective-permute-start = (bf16[1,128,160]{1,2,0:T(8,128)(2,1)S(1)}, bf16[1,128,160]{1,2,0:T(8,128)(2,1)S(1)}, u32[]{:S(2)}, u32[]{:S(2)}) collective-permute-start(bf16[1,128,160]{1,2,0:T(8,128)(2,1)S(1)} %get-tuple-element.27), channel_id=1, source_target_pairs={{0,2},{2,4},{4,6},{1,3},{3,5},{5,7},{8,10},{10,12},{12,14},{9,11},... | collective-permute-start | bytes 122888 | tf_op jit(solution)/shard_map/ppermute | solution.py:22
  6.1 1.3 %collective-permute-start.1 = (bf16[1,128,160]{1,2,0:T(8,128)(2,1)S(1)}, bf16[1,128,160]{1,2,0:T(8,128)(2,1)S(1)}, u32[]{:S(2)}, u32[]{:S(2)}) collective-permute-start(bf16[1,128,160]{1,2,0:T(8,128)(2,1)S(1)} %get-tuple-element.28), channel_id=1, source_target_pairs={{2,0},{4,2},{6,4},{3,1},{5,3},{7,5},{10,8},{12,10},{14,12},{11,9},... | collective-permute-start | bytes 122888 | tf_op jit(solution)/shard_map/ppermute | solution.py:24
  7.5 4.5 %collective-permute-start.6 = (bf16[1,128,160]{1,2,0:T(8,128)(2,1)S(1)}, bf16[1,128,160]{1,2,0:T(8,128)(2,1)S(1)}, u32[]{:S(2)}, u32[]{:S(2)}) collective-permute-start(bf16[1,128,160]{1,2,0:T(8,128)(2,1)S(1)} %get-tuple-element.33), channel_id=1, source_target_pairs={{0,2},{2,4},{4,6},{1,3},{3,5},{5,7},{8,10},{10,12},{12,14},{9,11},... | collective-permute-start | bytes 122888 | tf_op jit(solution)/shard_map/ppermute | solution.py:22
  12.0 0.0 copy-start.1
  12.0 1.6 %collective-permute-start.7 = (bf16[1,128,160]{1,2,0:T(8,128)(2,1)S(1)}, bf16[1,128,160]{1,2,0:T(8,128)(2,1)S(1)}, u32[]{:S(2)}, u32[]{:S(2)}) collective-permute-start(bf16[1,128,160]{1,2,0:T(8,128)(2,1)S(1)} %get-tuple-element.34), channel_id=1, source_target_pairs={{2,0},{4,2},{6,4},{3,1},{5,3},{7,5},{10,8},{12,10},{14,12},{11,9},... | collective-permute-start | bytes 122888 | tf_op jit(solution)/shard_map/ppermute | solution.py:24
  13.6 2.4 %fusion.112 = (bf16[3,3,160,640]{3,2,1,0:T(8,128)(2,1)S(1)}, bf16[3,3,160,640]{3,2,1,0:T(8,128)(2,1)S(1)}) fusion(bf16[3,3,160,1280]{3,2,1,0:T(8,128)(2,1)} %param.24), kind=kLoop, calls=%fused_computation.186 | loop fusion | bytes 7372800 | tf_op jit(solution)/shard_map/dynamic_slice | solution.py:41
  16.0 0.0 copy-start.7
  16.1 0.3 fusion.111
  16.4 0.3 copy-done.7
  16.7 0.0 copy-done.8
  16.7 0.0 copy-done.9
  16.7 0.0 copy-done.10
  16.7 0.0 copy-done.11
  16.7 0.0 copy-done.12
  16.7 1.4 %collective-permute-done.7 = bf16[1,128,160]{1,2,0:T(8,128)(2,1)S(1)} collective-permute-done((bf16[1,128,160]{1,2,0:T(8,128)(2,1)S(1)}, bf16[1,128,160]{1,2,0:T(8,128)(2,1)S(1)}, u32[]{:S(2)}, u32[]{:S(2)}) %collective-permute-start.7) | collective-permute-done | bytes 40992 | tf_op jit(solution)/shard_map/ppermute | solution.py:24
  18.2 7.9 %all-gather.3 = bf16[16,128,160]{1,2,0:T(8,128)(2,1)S(1)} all-gather(bf16[4,128,160]{1,2,0:T(8,128)(2,1)S(1)} %pad_maximum_fusion.3), channel_id=5, replica_groups=mesh['groups'=2,'section'=2,'band'=4,'chan'=2] {'section','chan'}, dimensions={0}, use_global_device_ids=true | all-gather | bytes 819200 | tf_op jit(solution)/shard_map/all_gather | solution.py:10
  26.2 8.0 %all-gather = bf16[16,128,160]{1,2,0:T(8,128)(2,1)S(1)} all-gather(bf16[4,128,160]{1,2,0:T(8,128)(2,1)S(1)} %pad_maximum_fusion), channel_id=2, replica_groups=mesh['groups'=2,'section'=2,'band'=4,'chan'=2] {'section','chan'}, dimensions={0}, use_global_device_ids=true | all-gather | bytes 819200 | tf_op jit(solution)/shard_map/all_gather | solution.py:10
  34.3 1.3 %fusion.120 = f32[4,128,1440]{1,2,0:T(8,128)S(1)} fusion(bf16[640,1440,1]{0,1,2:T(8,128)(2,1)S(1)} %bitcast.80, bf16[4,128,640]{1,2,0:T(8,128)(2,1)S(1)} %bitcast.95), kind=kOutput, calls=%fused_computation.194 | convolution fusion | flops 943718400 | bytes 5447680 | tf_op jit(solution)/shard_map/dot_general | solution.py:43
  35.6 0.2 copy-done.4
  35.8 1.3 %fusion.123 = f32[4,128,1440]{1,2,0:T(8,128)S(1)} fusion(bf16[640,1440,1]{0,1,2:T(8,128)(2,1)S(1)} %bitcast.97, bf16[4,128,640]{1,2,0:T(8,128)(2,1)S(1)} %bitcast.92), kind=kOutput, calls=%fused_computation.197 | convolution fusion | flops 943718400 | bytes 5447680 | tf_op jit(solution)/shard_map/dot_general | solution.py:43
  37.1 0.6 fusion.73
  37.8 3.6 %collective-permute-start.8 = (bf16[1,128,160]{1,2,0:T(8,128)(2,1)S(1)}, bf16[1,128,160]{1,2,0:T(8,128)(2,1)S(1)}, u32[]{:S(2)}, u32[]{:S(2)}) collective-permute-start(bf16[1,128,160]{1,2,0:T(8,128)(2,1)S(1)} %get-tuple-element.31), channel_id=1, source_target_pairs={{0,2},{2,4},{4,6},{1,3},{3,5},{5,7},{8,10},{10,12},{12,14},{9,11},... | collective-permute-start | bytes 122888 | tf_op jit(solution)/shard_map/ppermute | solution.py:22
  41.4 1.3 %collective-permute-start.9 = (bf16[1,128,160]{1,2,0:T(8,128)(2,1)S(1)}, bf16[1,128,160]{1,2,0:T(8,128)(2,1)S(1)}, u32[]{:S(2)}, u32[]{:S(2)}) collective-permute-start(bf16[1,128,160]{1,2,0:T(8,128)(2,1)S(1)} %get-tuple-element.32), channel_id=1, source_target_pairs={{2,0},{4,2},{6,4},{3,1},{5,3},{7,5},{10,8},{12,10},{14,12},{11,9},... | collective-permute-start | bytes 122888 | tf_op jit(solution)/shard_map/ppermute | solution.py:24
  42.7 4.5 %collective-permute-start.2 = (bf16[1,128,160]{1,2,0:T(8,128)(2,1)S(1)}, bf16[1,128,160]{1,2,0:T(8,128)(2,1)S(1)}, u32[]{:S(2)}, u32[]{:S(2)}) collective-permute-start(bf16[1,128,160]{1,2,0:T(8,128)(2,1)S(1)} %get-tuple-element.23), channel_id=1, source_target_pairs={{0,2},{2,4},{4,6},{1,3},{3,5},{5,7},{8,10},{10,12},{12,14},{9,11},... | collective-permute-start | bytes 122888 | tf_op jit(solution)/shard_map/ppermute | solution.py:22
  47.3 1.3 %collective-permute-start.3 = (bf16[1,128,160]{1,2,0:T(8,128)(2,1)S(1)}, bf16[1,128,160]{1,2,0:T(8,128)(2,1)S(1)}, u32[]{:S(2)}, u32[]{:S(2)}) collective-permute-start(bf16[1,128,160]{1,2,0:T(8,128)(2,1)S(1)} %get-tuple-element.24), channel_id=1, source_target_pairs={{2,0},{4,2},{6,4},{3,1},{5,3},{7,5},{10,8},{12,10},{14,12},{11,9},... | collective-permute-start | bytes 122888 | tf_op jit(solution)/shard_map/ppermute | solution.py:24
  48.6 7.2 %all-gather.4 = bf16[16,128,160]{1,2,0:T(8,128)(2,1)S(1)} all-gather(bf16[4,128,160]{1,2,0:T(8,128)(2,1)S(1)} %pad_maximum_fusion.4), channel_id=6, replica_groups=mesh['groups'=2,'section'=2,'band'=4,'chan'=2] {'section','chan'}, dimensions={0}, use_global_device_ids=true | all-gather | bytes 819200 | tf_op jit(solution)/shard_map/all_gather | solution.py:10
  55.9 8.0 %all-gather.1 = bf16[16,128,160]{1,2,0:T(8,128)(2,1)S(1)} all-gather(bf16[4,128,160]{1,2,0:T(8,128)(2,1)S(1)} %pad_maximum_fusion.1), channel_id=3, replica_groups=mesh['groups'=2,'section'=2,'band'=4,'chan'=2] {'section','chan'}, dimensions={0}, use_global_device_ids=true | all-gather | bytes 819200 | tf_op jit(solution)/shard_map/all_gather | solution.py:10
  63.9 1.3 %fusion.121 = f32[4,128,1440]{1,2,0:T(8,128)S(1)} fusion(bf16[640,1440,1]{0,1,2:T(8,128)(2,1)S(1)} %bitcast.98, bf16[4,128,640]{1,2,0:T(8,128)(2,1)S(1)} %bitcast.96), kind=kOutput, calls=%fused_computation.195 | convolution fusion | flops 943718400 | bytes 5447680 | tf_op jit(solution)/shard_map/dot_general | solution.py:43
  65.2 0.4 fusion.79
  65.6 4.5 %collective-permute-start.4 = (bf16[1,128,160]{1,2,0:T(8,128)(2,1)S(1)}, bf16[1,128,160]{1,2,0:T(8,128)(2,1)S(1)}, u32[]{:S(2)}, u32[]{:S(2)}) collective-permute-start(bf16[1,128,160]{1,2,0:T(8,128)(2,1)S(1)} %get-tuple-element.21), channel_id=1, source_target_pairs={{0,2},{2,4},{4,6},{1,3},{3,5},{5,7},{8,10},{10,12},{12,14},{9,11},... | collective-permute-start | bytes 122888 | tf_op jit(solution)/shard_map/ppermute | solution.py:22
  70.1 1.3 %collective-permute-start.5 = (bf16[1,128,160]{1,2,0:T(8,128)(2,1)S(1)}, bf16[1,128,160]{1,2,0:T(8,128)(2,1)S(1)}, u32[]{:S(2)}, u32[]{:S(2)}) collective-permute-start(bf16[1,128,160]{1,2,0:T(8,128)(2,1)S(1)} %get-tuple-element.22), channel_id=1, source_target_pairs={{2,0},{4,2},{6,4},{3,1},{5,3},{7,5},{10,8},{12,10},{14,12},{11,9},... | collective-permute-start | bytes 122888 | tf_op jit(solution)/shard_map/ppermute | solution.py:24
  71.4 1.3 %fusion.124 = f32[4,128,1440]{1,2,0:T(8,128)S(1)} fusion(bf16[640,1440,1]{0,1,2:T(8,128)(2,1)S(1)} %bitcast.99, bf16[4,128,640]{1,2,0:T(8,128)(2,1)S(1)} %bitcast.91), kind=kOutput, calls=%fused_computation.198 | convolution fusion | flops 943718400 | bytes 5447680 | tf_op jit(solution)/shard_map/dot_general | solution.py:43
  72.7 0.4 fusion.69
  73.1 6.1 %all_gather.49 = bf16[2,128,640]{1,2,0:T(8,128)(2,1)S(1)} all-gather(bf16[2,128,160]{1,2,0:T(8,128)(2,1)S(1)} %fusion.69), channel_id=1, replica_groups=mesh['groups'=2,'section'=2,'band'=4,'chan'=2] {'section','chan'}, dimensions={2}, use_global_device_ids=true | all-gather | bytes 409600 | tf_op jit(solution)/shard_map/all_gather | solution.py:104
  79.2 1.3 %collective-permute-start.11 = (bf16[1,128,640]{1,2,0:T(8,128)(2,1)S(1)}, bf16[1,128,640]{1,2,0:T(8,128)(2,1)S(1)}, u32[]{:S(2)}, u32[]{:S(2)}) collective-permute-start(bf16[1,128,640]{1,2,0:T(8,128)(2,1)S(1)} %get-tuple-element.17), channel_id=1, source_target_pairs={{2,0},{4,2},{6,4},{3,1},{5,3},{7,5},{10,8},{12,10},{14,12},{11,9},... | collective-permute-start | bytes 491528 | tf_op jit(solution)/shard_map/ppermute | solution.py:24
  80.5 5.2 %collective-permute-start.10 = (bf16[1,128,640]{1,2,0:T(8,128)(2,1)S(1)}, bf16[1,128,640]{1,2,0:T(8,128)(2,1)S(1)}, u32[]{:S(2)}, u32[]{:S(2)}) collective-permute-start(bf16[1,128,640]{1,2,0:T(8,128)(2,1)S(1)} %get-tuple-element.18), channel_id=1, source_target_pairs={{0,2},{2,4},{4,6},{1,3},{3,5},{5,7},{8,10},{10,12},{12,14},{9,11},... | collective-permute-start | bytes 491528 | tf_op jit(solution)/shard_map/ppermute | solution.py:22
  85.8 7.7 %all-gather.2 = bf16[16,128,160]{1,2,0:T(8,128)(2,1)S(1)} all-gather(bf16[4,128,160]{1,2,0:T(8,128)(2,1)S(1)} %pad_maximum_fusion.2), channel_id=4, replica_groups=mesh['groups'=2,'section'=2,'band'=4,'chan'=2] {'section','chan'}, dimensions={0}, use_global_device_ids=true | all-gather | bytes 819200 | tf_op jit(solution)/shard_map/all_gather | solution.py:10
  93.6 1.3 %fusion.122 = f32[4,128,1440]{1,2,0:T(8,128)S(1)} fusion(bf16[640,1440,1]{0,1,2:T(8,128)(2,1)S(1)} %bitcast.90, bf16[4,128,640]{1,2,0:T(8,128)(2,1)S(1)} %bitcast.94), kind=kOutput, calls=%fused_computation.196 | convolution fusion | flops 943718400 | bytes 5447680 | tf_op jit(solution)/shard_map/dot_general | solution.py:43
  95.0 1.3 %fusion.125 = f32[4,128,1440]{1,2,0:T(8,128)S(1)} fusion(bf16[640,1440,1]{0,1,2:T(8,128)(2,1)S(1)} %bitcast.89, bf16[4,128,640]{1,2,0:T(8,128)(2,1)S(1)} %constant_dynamic-update-slice_fusion), kind=kOutput, calls=%fused_computation.199 | convolution fusion | flops 943718400 | bytes 5447680 | tf_op jit(solution)/shard_map/dot_general | solution.py:43
  96.3 0.6 fusion.97
  97.0 3.9 %collective-permute-start.12 = (bf16[1,128,160]{1,2,0:T(8,128)(2,1)S(1)}, bf16[1,128,160]{1,2,0:T(8,128)(2,1)S(1)}, u32[]{:S(2)}, u32[]{:S(2)}) collective-permute-start(bf16[1,128,160]{1,2,0:T(8,128)(2,1)S(1)} %get-tuple-element.19), channel_id=1, source_target_pairs={{0,2},{2,4},{4,6},{1,3},{3,5},{5,7},{8,10},{10,12},{12,14},{9,11},... | collective-permute-start | bytes 122888 | tf_op jit(solution)/shard_map/ppermute | solution.py:22
  100.9 1.5 %collective-permute-start.13 = (bf16[1,128,160]{1,2,0:T(8,128)(2,1)S(1)}, bf16[1,128,160]{1,2,0:T(8,128)(2,1)S(1)}, u32[]{:S(2)}, u32[]{:S(2)}) collective-permute-start(bf16[1,128,160]{1,2,0:T(8,128)(2,1)S(1)} %get-tuple-element.20), channel_id=1, source_target_pairs={{2,0},{4,2},{6,4},{3,1},{5,3},{7,5},{10,8},{12,10},{14,12},{11,9},... | collective-permute-start | bytes 122888 | tf_op jit(solution)/shard_map/ppermute | solution.py:24
  102.4 1.3 %fusion.127 = f32[4,128,1440]{1,2,0:T(8,128)S(1)} fusion(bf16[640,1440,1]{0,1,2:T(8,128)(2,1)S(1)} %bitcast.88, bf16[4,128,640]{1,2,0:T(8,128)(2,1)S(1)} %constant_dynamic-update-slice_fusion), kind=kOutput, calls=%fused_computation.201 | convolution fusion | flops 943718400 | bytes 5447680 | tf_op jit(solution)/shard_map/dot_general | solution.py:43
  103.7 3.3 %collective-permute-done.13 = bf16[1,128,160]{1,2,0:T(8,128)(2,1)S(1)} collective-permute-done((bf16[1,128,160]{1,2,0:T(8,128)(2,1)S(1)}, bf16[1,128,160]{1,2,0:T(8,128)(2,1)S(1)}, u32[]{:S(2)}, u32[]{:S(2)}) %collective-permute-start.13) | collective-permute-done | bytes 40992 | tf_op jit(solution)/shard_map/ppermute | solution.py:24
  107.0 7.4 %all-gather.5 = bf16[16,128,160]{1,2,0:T(8,128)(2,1)S(1)} all-gather(bf16[4,128,160]{1,2,0:T(8,128)(2,1)S(1)} %pad_maximum_fusion.5), channel_id=7, replica_groups=mesh['groups'=2,'section'=2,'band'=4,'chan'=2] {'section','chan'}, dimensions={0}, use_global_device_ids=true | all-gather | bytes 819200 | tf_op jit(solution)/shard_map/all_gather | solution.py:10
  114.5 1.3 %fusion.126 = f32[4,128,1440]{1,2,0:T(8,128)S(1)} fusion(bf16[640,1440,1]{0,1,2:T(8,128)(2,1)S(1)} %bitcast.87, bf16[4,128,640]{1,2,0:T(8,128)(2,1)S(1)} %bitcast.93), kind=kOutput, calls=%fused_computation.200 | convolution fusion | flops 943718400 | bytes 5447680 | tf_op jit(solution)/shard_map/dot_general | solution.py:43
  115.8 1.2 %fusion.99 = bf16[2,128,160]{1,2,0:T(8,128)(2,1)} fusion(bf16[2,128,160]{1,2,0:T(8,128)(2,1)S(1)} %get-tuple-element.6, f32[4,128,1440]{1,2,0:T(8,128)S(1)} %fusion.127, f32[4,128,1440]{1,2,0:T(8,128)S(1)} %fusion.126, f32[160]{0:T(256)S(1)} %convert_element_type.126), kind=kLoop, calls=%fused_computation.168 | loop fusion | flops 860160 | bytes 7046144 | tf_op jit(solution)/shard_map/convert_element_type | solution.py:77
  (57 shorter events, 0.6 us)
Async XLA Ops:
  0.0 34.2 %copy-start = (bf16[3,3,160,640]{3,2,1,0:T(8,128)(2,1)S(1)}, bf16[3,3,160,640]{3,2,1,0:T(8,128)(2,1)}, u32[]{:S(2)}) copy-start(bf16[3,3,160,640]{3,2,1,0:T(8,128)(2,1)} %param.20) | copy-start | bytes 5529604
  1.2 25.0 %collective-permute-start = (bf16[1,128,160]{1,2,0:T(8,128)(2,1)S(1)}, bf16[1,128,160]{1,2,0:T(8,128)(2,1)S(1)}, u32[]{:S(2)}, u32[]{:S(2)}) collective-permute-start(bf16[1,128,160]{1,2,0:T(8,128)(2,1)S(1)} %get-tuple-element.27), channel_id=1, source_target_pairs={{0,2},{2,4},{4,6},{1,3},{3,5},{5,7},{8,10},{10,12},{12,14},{9,11},... | collective-permute-start | bytes 122888 | tf_op jit(solution)/shard_map/ppermute | solution.py:22
  6.1 20.0 %collective-permute-start.1 = (bf16[1,128,160]{1,2,0:T(8,128)(2,1)S(1)}, bf16[1,128,160]{1,2,0:T(8,128)(2,1)S(1)}, u32[]{:S(2)}, u32[]{:S(2)}) collective-permute-start(bf16[1,128,160]{1,2,0:T(8,128)(2,1)S(1)} %get-tuple-element.28), channel_id=1, source_target_pairs={{2,0},{4,2},{6,4},{3,1},{5,3},{7,5},{10,8},{12,10},{14,12},{11,9},... | collective-permute-start | bytes 122888 | tf_op jit(solution)/shard_map/ppermute | solution.py:24
  7.5 9.3 %collective-permute-start.6 = (bf16[1,128,160]{1,2,0:T(8,128)(2,1)S(1)}, bf16[1,128,160]{1,2,0:T(8,128)(2,1)S(1)}, u32[]{:S(2)}, u32[]{:S(2)}) collective-permute-start(bf16[1,128,160]{1,2,0:T(8,128)(2,1)S(1)} %get-tuple-element.33), channel_id=1, source_target_pairs={{0,2},{2,4},{4,6},{1,3},{3,5},{5,7},{8,10},{10,12},{12,14},{9,11},... | collective-permute-start | bytes 122888 | tf_op jit(solution)/shard_map/ppermute | solution.py:22
  12.0 4.0 %copy-start.1 = (bf16[3,3,160,1280]{3,2,1,0:T(8,128)(2,1)S(1)}, bf16[3,3,160,1280]{3,2,1,0:T(8,128)(2,1)}, u32[]{:S(2)}) copy-start(bf16[3,3,160,1280]{3,2,1,0:T(8,128)(2,1)} %param.26) | copy-start | bytes 11059204
  12.0 6.2 %collective-permute-start.7 = (bf16[1,128,160]{1,2,0:T(8,128)(2,1)S(1)}, bf16[1,128,160]{1,2,0:T(8,128)(2,1)S(1)}, u32[]{:S(2)}, u32[]{:S(2)}) collective-permute-start(bf16[1,128,160]{1,2,0:T(8,128)(2,1)S(1)} %get-tuple-element.34), channel_id=1, source_target_pairs={{2,0},{4,2},{6,4},{3,1},{5,3},{7,5},{10,8},{12,10},{14,12},{11,9},... | collective-permute-start | bytes 122888 | tf_op jit(solution)/shard_map/ppermute | solution.py:24
  16.0 0.7 copy-start.7
  16.0 0.7 copy-start.8
  16.0 0.7 copy-start.9
  16.0 0.7 copy-start.10
  16.0 0.7 copy-start.11
  16.0 0.7 copy-start.12
  34.3 1.5 %copy-start.4 = (bf16[3,3,160,640]{3,2,1,0:T(8,128)(2,1)S(1)}, bf16[3,3,160,640]{3,2,1,0:T(8,128)(2,1)}, u32[]{:S(2)}) copy-start(bf16[3,3,160,640]{3,2,1,0:T(8,128)(2,1)} %param.16) | copy-start | bytes 5529604
  35.6 1.5 %copy-start.2 = (bf16[2,128,160]{1,2,0:T(8,128)(2,1)S(1)}, bf16[2,128,160]{1,2,0:T(8,128)(2,1)}, u32[]{:S(2)}) copy-start(bf16[2,128,160]{1,2,0:T(8,128)(2,1)} %param.14) | copy-start | bytes 245764
  35.6 1.5 %copy-start.3 = (bf16[2,128,160]{1,2,0:T(8,128)(2,1)S(1)}, bf16[2,128,160]{1,2,0:T(8,128)(2,1)}, u32[]{:S(2)}) copy-start(bf16[2,128,160]{1,2,0:T(8,128)(2,1)} %param.15) | copy-start | bytes 245764
  37.7 26.2 %copy-start.5 = (bf16[3,3,160,640]{3,2,1,0:T(8,128)(2,1)S(1)}, bf16[3,3,160,640]{3,2,1,0:T(8,128)(2,1)}, u32[]{:S(2)}) copy-start(bf16[3,3,160,640]{3,2,1,0:T(8,128)(2,1)} %param.22) | copy-start | bytes 5529604
  37.8 10.8 %collective-permute-start.8 = (bf16[1,128,160]{1,2,0:T(8,128)(2,1)S(1)}, bf16[1,128,160]{1,2,0:T(8,128)(2,1)S(1)}, u32[]{:S(2)}, u32[]{:S(2)}) collective-permute-start(bf16[1,128,160]{1,2,0:T(8,128)(2,1)S(1)} %get-tuple-element.31), channel_id=1, source_target_pairs={{0,2},{2,4},{4,6},{1,3},{3,5},{5,7},{8,10},{10,12},{12,14},{9,11},... | collective-permute-start | bytes 122888 | tf_op jit(solution)/shard_map/ppermute | solution.py:22
  41.4 7.2 %collective-permute-start.9 = (bf16[1,128,160]{1,2,0:T(8,128)(2,1)S(1)}, bf16[1,128,160]{1,2,0:T(8,128)(2,1)S(1)}, u32[]{:S(2)}, u32[]{:S(2)}) collective-permute-start(bf16[1,128,160]{1,2,0:T(8,128)(2,1)S(1)} %get-tuple-element.32), channel_id=1, source_target_pairs={{2,0},{4,2},{6,4},{3,1},{5,3},{7,5},{10,8},{12,10},{14,12},{11,9},... | collective-permute-start | bytes 122888 | tf_op jit(solution)/shard_map/ppermute | solution.py:24
  42.7 13.1 %collective-permute-start.2 = (bf16[1,128,160]{1,2,0:T(8,128)(2,1)S(1)}, bf16[1,128,160]{1,2,0:T(8,128)(2,1)S(1)}, u32[]{:S(2)}, u32[]{:S(2)}) collective-permute-start(bf16[1,128,160]{1,2,0:T(8,128)(2,1)S(1)} %get-tuple-element.23), channel_id=1, source_target_pairs={{0,2},{2,4},{4,6},{1,3},{3,5},{5,7},{8,10},{10,12},{12,14},{9,11},... | collective-permute-start | bytes 122888 | tf_op jit(solution)/shard_map/ppermute | solution.py:22
  47.3 8.6 %collective-permute-start.3 = (bf16[1,128,160]{1,2,0:T(8,128)(2,1)S(1)}, bf16[1,128,160]{1,2,0:T(8,128)(2,1)S(1)}, u32[]{:S(2)}, u32[]{:S(2)}) collective-permute-start(bf16[1,128,160]{1,2,0:T(8,128)(2,1)S(1)} %get-tuple-element.24), channel_id=1, source_target_pairs={{2,0},{4,2},{6,4},{3,1},{5,3},{7,5},{10,8},{12,10},{14,12},{11,9},... | collective-permute-start | bytes 122888 | tf_op jit(solution)/shard_map/ppermute | solution.py:24
  65.2 6.2 %copy-start.6 = (bf16[3,3,160,640]{3,2,1,0:T(8,128)(2,1)S(1)}, bf16[3,3,160,640]{3,2,1,0:T(8,128)(2,1)}, u32[]{:S(2)}) copy-start(bf16[3,3,160,640]{3,2,1,0:T(8,128)(2,1)} %param.18) | copy-start | bytes 5529604
  65.6 20.1 %collective-permute-start.4 = (bf16[1,128,160]{1,2,0:T(8,128)(2,1)S(1)}, bf16[1,128,160]{1,2,0:T(8,128)(2,1)S(1)}, u32[]{:S(2)}, u32[]{:S(2)}) collective-permute-start(bf16[1,128,160]{1,2,0:T(8,128)(2,1)S(1)} %get-tuple-element.21), channel_id=1, source_target_pairs={{0,2},{2,4},{4,6},{1,3},{3,5},{5,7},{8,10},{10,12},{12,14},{9,11},... | collective-permute-start | bytes 122888 | tf_op jit(solution)/shard_map/ppermute | solution.py:22
  70.1 15.6 %collective-permute-start.5 = (bf16[1,128,160]{1,2,0:T(8,128)(2,1)S(1)}, bf16[1,128,160]{1,2,0:T(8,128)(2,1)S(1)}, u32[]{:S(2)}, u32[]{:S(2)}) collective-permute-start(bf16[1,128,160]{1,2,0:T(8,128)(2,1)S(1)} %get-tuple-element.22), channel_id=1, source_target_pairs={{2,0},{4,2},{6,4},{3,1},{5,3},{7,5},{10,8},{12,10},{14,12},{11,9},... | collective-permute-start | bytes 122888 | tf_op jit(solution)/shard_map/ppermute | solution.py:24
  79.2 15.7 %collective-permute-start.11 = (bf16[1,128,640]{1,2,0:T(8,128)(2,1)S(1)}, bf16[1,128,640]{1,2,0:T(8,128)(2,1)S(1)}, u32[]{:S(2)}, u32[]{:S(2)}) collective-permute-start(bf16[1,128,640]{1,2,0:T(8,128)(2,1)S(1)} %get-tuple-element.17), channel_id=1, source_target_pairs={{2,0},{4,2},{6,4},{3,1},{5,3},{7,5},{10,8},{12,10},{14,12},{11,9},... | collective-permute-start | bytes 491528 | tf_op jit(solution)/shard_map/ppermute | solution.py:24
  80.5 14.4 %collective-permute-start.10 = (bf16[1,128,640]{1,2,0:T(8,128)(2,1)S(1)}, bf16[1,128,640]{1,2,0:T(8,128)(2,1)S(1)}, u32[]{:S(2)}, u32[]{:S(2)}) collective-permute-start(bf16[1,128,640]{1,2,0:T(8,128)(2,1)S(1)} %get-tuple-element.18), channel_id=1, source_target_pairs={{0,2},{2,4},{4,6},{1,3},{3,5},{5,7},{8,10},{10,12},{12,14},{9,11},... | collective-permute-start | bytes 491528 | tf_op jit(solution)/shard_map/ppermute | solution.py:22
  97.0 6.7 %collective-permute-start.12 = (bf16[1,128,160]{1,2,0:T(8,128)(2,1)S(1)}, bf16[1,128,160]{1,2,0:T(8,128)(2,1)S(1)}, u32[]{:S(2)}, u32[]{:S(2)}) collective-permute-start(bf16[1,128,160]{1,2,0:T(8,128)(2,1)S(1)} %get-tuple-element.19), channel_id=1, source_target_pairs={{0,2},{2,4},{4,6},{1,3},{3,5},{5,7},{8,10},{10,12},{12,14},{9,11},... | collective-permute-start | bytes 122888 | tf_op jit(solution)/shard_map/ppermute | solution.py:22
  100.9 6.1 %collective-permute-start.13 = (bf16[1,128,160]{1,2,0:T(8,128)(2,1)S(1)}, bf16[1,128,160]{1,2,0:T(8,128)(2,1)S(1)}, u32[]{:S(2)}, u32[]{:S(2)}) collective-permute-start(bf16[1,128,160]{1,2,0:T(8,128)(2,1)S(1)} %get-tuple-element.20), channel_id=1, source_target_pairs={{2,0},{4,2},{6,4},{3,1},{5,3},{7,5},{10,8},{12,10},{14,12},{11,9},... | collective-permute-start | bytes 122888 | tf_op jit(solution)/shard_map/ppermute | solution.py:24
